TPU v7x, 256 devices: a whole 4x4x8 slice. The times are simulated.
256 devices in a mesh: outer: 8 (over x, y_lo), inner: 8 (over z), tensor: 4 (over y_hi, core).
Axes of the slice: x: 4, y: 4 (y_hi: 2, y_lo: 2; y = y_hi * 2 + y_lo), z: 8, core: 2. Of those that a mesh axis runs over, the one named last changes fastest.
Arguments:
- queries: bfloat16 [16384, 16, 128], P(('outer', 'inner'), 'tensor'), may hold values from -5 to 5
- keys: bfloat16 [16384, 4, 128], P(('outer', 'inner'), 'tensor'), may hold values from -5 to 5
- values: bfloat16 [16384, 4, 128], P(('outer', 'inner'), 'tensor'), may hold values from -6 to 6
- w_out: bfloat16 [16, 128, 4096], P('tensor'), may hold values from -0.125 to 0.125
- d_out: bfloat16 [16384, 4096], P(('outer', 'inner', 'tensor')), may hold values from -6 to 6
- lengths: int32 [16], replicated, may hold values from 1 to 10240, 16384 in all
Outputs:
- mixed: bfloat16 [16384, 4096], P(('outer', 'inner', 'tensor'))
- d_queries: bfloat16 [16384, 16, 128], P(('outer', 'inner'), 'tensor')
- d_keys: bfloat16 [16384, 4, 128], P(('outer', 'inner'), 'tensor')
- d_values: bfloat16 [16384, 4, 128], P(('outer', 'inner'), 'tensor')
Inputs may be any that keep to these rules, and one draw needn't show every extreme that they name: `lengths`: the 16 documents fill the sequence of 16384 tokens exactly, and the longest has exactly 10240 tokens.
All inputs are finite; a program needn't handle non-finite values.
Results may differ from a plain program's by a relative error of at most 0.04.
Values may be sent and summed in bfloat16 or wider, within the bound.
A program may use at most 128 MiB of HBM per device.

v0:
```python
import jax
import jax.numpy as jnp
from jax import lax
from jax.sharding import PartitionSpec as P

NEG_FILL = -1e30


def segment_of(positions, ends):
    return jnp.sum((positions[:, None] >= ends[None, :]).astype(jnp.int32), axis=1)


def doc_begin(position, ends):
    return jnp.max(jnp.where(ends <= position, ends, jnp.zeros_like(ends)))


def masked_scores(q_rows, k_block, q_pos, q_seg, k_start, ends, scale):
    width = k_block.shape[0]
    k_pos = k_start + jnp.arange(width, dtype=jnp.int32)
    k_seg = segment_of(k_pos, ends)
    s = (
        lax.dot_general(
            q_rows, k_block, (((1,), (1,)), ((), ())), preferred_element_type=jnp.float32
        )
        * scale
    )
    mask = (k_pos[None, :] <= q_pos[:, None]) & (k_seg[None, :] == q_seg[:, None])
    return (jnp.where(mask, s, NEG_FILL), mask)


def local(queries, keys, values, w_out, d_out, lengths):
    tok, heads_here, head_dim = queries.shape
    kv_here = keys.shape[1]
    group = heads_here // kv_here
    width = w_out.shape[2]
    ctx = lax.axis_size(("outer", "inner"))
    total = tok * ctx
    scale = head_dim ** (-0.5)
    offset = lax.axis_index(("outer", "inner")) * tok
    ends = jnp.cumsum(lengths)
    first = doc_begin(offset, ends)
    last = offset + tok - 1
    factor = 1
    while factor < ctx and tok * factor < 1024 and (ctx % (factor * 2) == 0):
        factor = factor * 2
    span = tok * factor
    n_blocks = total // span
    q_pos = offset + jnp.arange(tok * group, dtype=jnp.int32) // group
    q_seg = segment_of(q_pos, ends)
    key_all, value_all = (
        lax.all_gather(keys, ("outer", "inner"), axis=0, tiled=True),
        lax.all_gather(values, ("outer", "inner"), axis=0, tiled=True),
    )
    q_groups = queries.reshape(tok, kv_here, group, head_dim)
    zero = jnp.zeros((), jnp.int32)

    def needed(k_start, k_width):
        return (k_start <= last) & (k_start + k_width - 1 >= first)

    q_list = [q_groups[:, 0].reshape(tok * group, head_dim)]
    lse_list = []
    c = 0
    q_rows = q_list[c]

    def forward_block(b, carry, q_rows=q_rows, c=c):
        k_start = b * span

        def forward_work(state):
            top, denom, acc = state
            k_block = lax.dynamic_slice_in_dim(key_all, k_start, span, 0)[:, c]
            v_block = lax.dynamic_slice_in_dim(value_all, k_start, span, 0)[:, c]
            s, mask = masked_scores(q_rows, k_block, q_pos, q_seg, k_start, ends, scale)
            new_top = jnp.maximum(top, jnp.max(s, axis=1))
            weights = jnp.where(mask, jnp.exp(s - new_top[:, None]), 0.0)
            shrink = jnp.exp(top - new_top)
            denom = denom * shrink + jnp.sum(weights, axis=1)
            acc = acc * shrink[:, None] + jnp.dot(
                weights.astype(jnp.bfloat16), v_block, preferred_element_type=jnp.float32
            )
            return (new_top, denom, acc)

        return lax.cond(needed(k_start, span), forward_work, lambda st: st, carry)

    start_state = (
        jnp.full((tok * group,), NEG_FILL, jnp.float32),
        jnp.zeros((tok * group,), jnp.float32),
        jnp.zeros((tok * group, head_dim), jnp.float32),
    )
    top, denom, acc = lax.fori_loop(0, n_blocks, forward_block, start_state)
    attn_parts = [(acc / denom[:, None]).astype(jnp.bfloat16).reshape(tok, group, head_dim)]
    lse_list.append(top + jnp.log(denom))
    attn = jnp.stack(attn_parts, axis=1).reshape(tok, heads_here * head_dim)
    w_flat = w_out.reshape(heads_here * head_dim, width)
    mixed = lax.psum_scatter(
        jnp.dot(attn, w_flat, preferred_element_type=jnp.float32).astype(jnp.bfloat16),
        "tensor",
        scatter_dimension=0,
        tiled=True,
    )
    d_attn = lax.dot_general(
        lax.all_gather(d_out, "tensor", axis=0, tiled=True),
        w_flat,
        (((1,), (1,)), ((), ())),
        preferred_element_type=jnp.float32,
    ).astype(jnp.bfloat16)
    d_groups = d_attn.reshape(tok, kv_here, group, head_dim)
    a_groups = attn.reshape(tok, kv_here, group, head_dim)
    deltas = jnp.sum(d_groups.astype(jnp.float32) * a_groups.astype(jnp.float32), axis=3)
    g_list = [d_groups[:, 0].reshape(tok * group, head_dim)]
    delta_list = [deltas[:, 0].reshape(tok * group)]

    def grad_terms(c, k_start, k_width):
        k_block = lax.dynamic_slice_in_dim(key_all, k_start, k_width, 0)[:, c]
        v_block = lax.dynamic_slice_in_dim(value_all, k_start, k_width, 0)[:, c]
        s, mask = masked_scores(q_list[c], k_block, q_pos, q_seg, k_start, ends, scale)
        probs = jnp.where(mask, jnp.exp(s - lse_list[c][:, None]), 0.0)
        d_val = lax.dot_general(
            probs.astype(jnp.bfloat16),
            g_list[c],
            (((0,), (0,)), ((), ())),
            preferred_element_type=jnp.float32,
        )
        d_prob = lax.dot_general(
            g_list[c], v_block, (((1,), (1,)), ((), ())), preferred_element_type=jnp.float32
        )
        d_score = (probs * (d_prob - delta_list[c][:, None])).astype(jnp.bfloat16)
        dq_add = jnp.dot(d_score, k_block, preferred_element_type=jnp.float32) * scale
        d_key = (
            lax.dot_general(
                d_score, q_list[c], (((0,), (0,)), ((), ())), preferred_element_type=jnp.float32
            )
            * scale
        )
        return (dq_add, d_key, d_val)

    dq_start = tuple((jnp.zeros((tok * group, head_dim), jnp.float32) for c in range(kv_here)))

    def backward_block(b, carry):
        k_start = b * span

        def backward_work(state):
            dq_all, key_terms = state
            dq_add, d_key, d_val = grad_terms(0, k_start, span)
            new_dq = [dq_all[0] + dq_add]
            piece = jnp.stack((d_key, d_val), axis=1)[:, :, None, :]
            key_terms = lax.dynamic_update_slice(key_terms, piece, (k_start, zero, zero + 0, zero))
            return (tuple(new_dq), key_terms)

        return lax.cond(needed(k_start, span), backward_work, lambda st: st, carry)

    term_start = jnp.zeros((total, 2, kv_here, head_dim), jnp.float32)
    dq_all, key_terms = lax.fori_loop(0, n_blocks, backward_block, (dq_start, term_start))
    key_grads = lax.psum_scatter(key_terms, ("outer", "inner"), scatter_dimension=0, tiled=True)
    d_queries = (
        jnp.stack([d.reshape(tok, group, head_dim) for d in dq_all], axis=1)
        .reshape(tok, heads_here, head_dim)
        .astype(jnp.bfloat16)
    )
    d_keys = key_grads[:, 0].astype(jnp.bfloat16)
    d_values = key_grads[:, 1].astype(jnp.bfloat16)
    return (mixed, d_queries, d_keys, d_values)


def solution(mesh):
    return jax.shard_map(
        local,
        mesh=mesh,
        in_specs=(
            P(("outer", "inner"), "tensor", None),
            P(("outer", "inner"), "tensor", None),
            P(("outer", "inner"), "tensor", None),
            P("tensor", None, None),
            P(("outer", "inner", "tensor"), None),
            P(),
        ),
        out_specs=(
            P(("outer", "inner", "tensor"), None),
            P(("outer", "inner"), "tensor", None),
            P(("outer", "inner"), "tensor", None),
            P(("outer", "inner"), "tensor", None),
        ),
        check_vma=False,
    )
```

profile of v0, /device:TPU:1, one launch (start us, length us, event | category | flops | bytes accessed | tf_op | source)
XLA Modules:
  0.0 1239.3 jit_solution(10827884792633760065)
XLA Ops:
  7.2 0.0 all-gather.8.cloned.1.call-start
  7.2 0.7 all-gather.8.cloned.1.call-update
  7.9 0.0 all-gather.4.cloned.1.call-start
  7.9 0.7 all-gather.4.cloned.1.call-update
  8.6 0.0 all-gather.6.cloned.1.call-start
  8.7 0.7 all-gather.6.cloned.1.call-update
  9.4 0.0 reduce-scatter.5.cloned.1.call-start
  9.4 0.7 copy.16
  10.2 0.1 reduce.1
  10.3 0.6 fusion.57
  11.0 0.1 convert_reduce_fusion.2
  11.1 32.1 %all-gather.8.cloned.1.call-done = bf16[256,4096]{1,0:T(8,128)(2,1)} async-done(((bf16[64,4096]{1,0:T(8,128)(2,1)}), bf16[256,4096]{1,0:T(8,128)(2,1)}) %all-gather.8.cloned.1.call-update) | async-done | bytes 2097168 | tf_op jit(solution)/shard_map/all_gather | solution.py:101
  43.2 0.0 copy-start
  43.2 4.1 convolution_convert_fusion.1
  47.3 0.2 reshape_squeeze_reshape.7
  47.5 0.2 reshape.141
  47.7 253.0 %all-gather.4.cloned.1.call-done = bf16[16384,1,128]{2,0,1:T(8,128)(2,1)} async-done(((bf16[256,1,128]{2,0,1:T(8,128)(2,1)}), bf16[16384,1,128]{2,0,1:T(8,128)(2,1)}) %all-gather.4.cloned.1.call-update) | async-done | bytes 4194320 | tf_op jit(solution)/shard_map/all_gather | solution.py:51
  300.7 302.0 %all-gather.6.cloned.1.call-done = bf16[16384,1,128]{2,0,1:T(8,128)(2,1)} async-done(((bf16[256,1,128]{2,0,1:T(8,128)(2,1)}), bf16[16384,1,128]{2,0,1:T(8,128)(2,1)}) %all-gather.6.cloned.1.call-update) | async-done | bytes 4194320 | tf_op jit(solution)/shard_map/all_gather | solution.py:52
  602.7 0.0 copy-done
  602.7 17.8 %while.42 = (s32[]{:T(128)}, f32[1024]{0:T(1024)S(1)}, f32[1024]{0:T(1024)S(1)}, f32[1024,128]{1,0:T(8,128)S(1)}, s32[]{:T(128)}, /*index=5*/s32[]{:T(128)}, s32...) while((s32[]{:T(128)}, f32[1024]{0:T(1024)S(1)}, ...), condition=%wide.region_9.10_spmd.clone, body=%wide.region_3.9_spmd.clone.sunk | while | flops 560262144 | bytes 14574053 | solution.py:89
  603.3 6.7 conditional.6
  603.4 0.1 convert_reduce_fusion
  603.5 2.2 fusion.4
  605.7 1.6 fusion.6
  607.3 2.7 fusion.9
  620.5 0.2 divide_convert_fusion
  620.8 0.4 fusion.52
  621.2 6.0 broadcast_in_dim.31
  627.1 20.5 %while.43 = (s32[]{:T(128)}, f32[1024,128]{1,0:T(8,128)S(1)}, f32[16384,2,1,128]{3,0,1,2:T(8,128)}, s32[]{:T(128)}, s32[]{:T(128)}, /*index=5*/s32[16]{0:T(128)S...) while((s32[]{:T(128)}, f32[1024,128]{1,0:T(8,128)S(1)}, ...), condition=%wide.region_16.17_spmd.clone, body=%wide.region_12.16_spmd.clone.sunk | while | flops 1361765376 | bytes 24998396 | solution.py:152
  627.8 9.4 conditional.7
  627.8 0.1 sub.71
  628.0 0.1 convert_reduce_fusion.1
  628.0 1.7 fusion.39
  629.7 2.6 fusion.24
  632.3 1.3 fusion.31
  633.6 1.8 fusion.35
  635.4 0.7 fusion.34
  636.1 1.1 fusion.36
  647.6 0.0 reduce-scatter.5.cloned.1.call-update
  647.7 0.0 reduce-scatter.3.cloned.1.call-start
  647.7 0.2 reshape_stack_reshape.4
  647.9 4.8 convolution_convert_fusion
  652.7 0.0 reduce-scatter.3.cloned.1.call-update
  652.7 0.7 convert_element_type.119
  653.4 491.7 %reduce-scatter.5.cloned.1.call-done = f32[256,2,1,128]{3,0,2,1:T(8,128)} async-done(((f32[16384,2,1,128]{3,0,2,1:T(8,128)}), f32[256,2,1,128]{3,0,2,1:T(8,128)}) %reduce-scatter.5.cloned.1.call-update) | async-done | bytes 262160 | tf_op jit(solution)/shard_map/reduce_scatter | solution.py:153
  1145.1 1.0 convert.6
  1146.1 0.7 slice_bitcast_fusion
  1146.8 86.0 %reduce-scatter.3.cloned.1.call-done = bf16[64,4096]{1,0:T(8,128)(2,1)} async-done(((bf16[256,4096]{1,0:T(8,128)(2,1)}), bf16[64,4096]{1,0:T(8,128)(2,1)}) %reduce-scatter.3.cloned.1.call-update) | async-done | bytes 524304 | tf_op jit(solution)/shard_map/reduce_scatter | solution.py:94
  (106 shorter events, 0.9 us)
Async XLA Ops:
  7.2 36.0 %all-gather.8.cloned.1.call-start = ((), (), s32[]{:S(2)}) async-start(), calls=%async_computation.5 | async-start | bytes 2621440 | tf_op jit(solution)/shard_map/all_gather | solution.py:101
  7.9 292.8 %all-gather.4.cloned.1.call-start = ((), (), s32[]{:S(2)}) async-start(), calls=%async_computation.2 | async-start | bytes 4259840 | tf_op jit(solution)/shard_map/all_gather | solution.py:51
  8.6 594.0 %all-gather.6.cloned.1.call-start = ((), (), s32[]{:S(2)}) async-start(), calls=%async_computation.3 | async-start | bytes 4259840 | tf_op jit(solution)/shard_map/all_gather | solution.py:52
  9.4 1135.8 %reduce-scatter.5.cloned.1.call-start = ((), (), s32[]{:S(2)}) async-start(), calls=%async_computation.6 | async-start | bytes 17039360 | tf_op jit(solution)/shard_map/reduce_scatter | solution.py:153
  43.2 559.5 %copy-start = (bf16[256,4,128]{2,1,0:T(4,128)(2,1)S(1)}, bf16[256,4,128]{2,1,0:T(4,128)(2,1)}, u32[]{:S(2)}) copy-start(bf16[256,4,128]{2,1,0:T(4,128)(2,1)} %param.14) | copy-start | bytes 786436
  647.7 585.1 %reduce-scatter.3.cloned.1.call-start = ((), (), s32[]{:S(2)}) async-start(), calls=%async_computation.4 | async-start | bytes 2621440 | tf_op jit(solution)/shard_map/reduce_scatter | solution.py:94
Sparse Core Ops, SparseCore 0:
  9.8 33.3 all-gather.7
  45.0 255.6 all-gather.3
  302.5 300.1 all-gather.5
  647.8 497.3 reduce-scatter.4
  1148.3 84.3 reduce-scatter.2
where the time goes:
time: 1240 us
  waiting for transfers between devices  1170 us (94%)
  loops' own time  22.2 us (2%)
  matrix products  21.9 us (2%)
  between operations  13.9 us (1%)
    reduce_scatter x1, waiting for transfers between devices, local(): lax.psum_scatter(key_terms, ('outer', 'inner'), scatter_dimension=0, tile...  492 us
    all_gather x1, waiting for transfers between devices, local(): lax.all_gather(values, ('outer', 'inner'), axis=0, tiled=True)  302 us
    all_gather x1, waiting for transfers between devices, local(): lax.all_gather(keys, ('outer', 'inner'), axis=0, tiled=True)  253 us
    reduce_scatter x1, waiting for transfers between devices, local(): lax.psum_scatter(jnp.dot(attn, w_flat, preferred_element_type=jnp.float32...  86 us
    all_gather x1, waiting for transfers between devices, local(): lax.all_gather(d_out, 'tensor', axis=0, tiled=True)  32.1 us
  transfers between devices with their start and end apart: 5, of which 5 were waited for; matrix products, arithmetic and copies ran while one was open for 1% of the time, Pallas kernels for 0%

commit v1 on v0

v1 whole, which is shorter than its diff:
```python
import jax
import jax.numpy as jnp
from jax import lax
from jax.experimental import pallas as pl
from jax.experimental.pallas import tpu as pltpu
from jax.sharding import PartitionSpec as P

MESH = pl.DeviceIdType.MESH
NT = (((1,), (1,)), ((), ()))
NN = (((1,), (0,)), ((), ()))
TN = (((0,), (0,)), ((), ()))
F32, BF16 = jnp.float32, jnp.bfloat16
LOG2E = 1.4426950408889634
LOW, FLOOR = -1e30, -1e20
VMEM, ANY, SMEM = pltpu.VMEM, pl.ANY, pltpu.SMEM

NX, NY, NZ = 4, 2, 8
TOK = 256
SUB = TOK // NX
GROUP = 4
ROWS = TOK * GROUP
HD = 128
SHARDS = NX * NY * NZ
TILE = 256
RUNS = TILE // SUB
CHUNK = 256
SCALE = HD**-0.5


def place():
    outer, z, t = lax.axis_index("outer"), lax.axis_index("inner"), lax.axis_index("tensor")
    return outer // NY, outer % NY, z, t


def at(x, y, z, t):
    return {"outer": x * NY + y, "inner": z, "tensor": t}


def remote(src, dst, send, recv, device):
    return pltpu.make_async_remote_copy(
        src_ref=src, dst_ref=dst, send_sem=send, recv_sem=recv, device_id=device, device_id_type=MESH
    )


def meet(devices):
    barrier = pltpu.get_barrier_semaphore()
    for device in devices:
        pl.semaphore_signal(barrier, inc=1, device_id=device, device_id_type=MESH)
    pl.semaphore_wait(barrier, len(devices))


PLANE = [(dx, dy) for dy in range(NY) for dx in range(NX) if (dx, dy) != (0, 0)]


def gather_kernel(q, kv, do, qa, kva, doa, qs, qr, ks, kr, zs, zr, ds, dr, ls):
    x, y, z, t = place()
    right, left = (x + 1) % NX, (x + NX - 1) % NX
    up, down = (z + 1) % NZ, (z + NZ - 1) % NZ
    partner, far = t + 1 - 2 * (t % 2), (t + 2) % 4
    meet(
        [at((x + dx) % NX, (y + dy) % NY, z, t) for dx, dy in PLANE]
        + [at(x, y, up, t), at(x, y, down, t), at(x, y, z, partner), at(x, y, z, far)]
    )
    plane, landed = [], []
    for i, (dx, dy) in enumerate(PLANE):
        tx, ty = (x + dx) % NX, (y + dy) % NY
        fx, fy = (x + NX - dx) % NX, (y + NY - dy) % NY
        copy = remote(kv.at[:, tx], kva.at[:, x, y, z], ks.at[i], kr.at[i], at(tx, ty, z, t))
        copy.start()
        plane.append(copy)
        landed.append(remote(kv.at[:, tx], kva.at[:, fx, fy, z], ks.at[i], kr.at[i], at(tx, ty, z, t)))
    own_kv = pltpu.make_async_copy(kv.at[:, x], kva.at[:, x, y, z], ls.at[0])
    own_kv.start()
    far_do = remote(do, doa.at[t], ds.at[0], dr.at[0], at(x, y, z, far))
    near_do = remote(do, doa.at[t], ds.at[1], dr.at[1], at(x, y, z, partner))
    far_do.start()
    near_do.start()
    to_right = remote(q, qa.at[1], qs.at[0], qr.at[0], at(right, y, z, t))
    to_left = remote(q, qa.at[3], qs.at[1], qr.at[1], at(left, y, z, t))
    to_right.start()
    to_left.start()
    own_do = pltpu.make_async_copy(do, doa.at[t], ls.at[1])
    own_do.start()
    own_q = pltpu.make_async_copy(q, qa.at[0], ls.at[2])
    own_q.start()
    own_kv.wait()
    for copy in landed:
        copy.wait_recv()
    streams = [(0, 0, 4), (1, 1, 4), (0, 1, 3), (1, 0, 3)]
    sent = []

    def hop(step):
        for i, (half, way, hops) in enumerate(streams):
            if step < hops:
                block = (z + NZ - step) % NZ if way == 0 else (z + step) % NZ
                part = kva.at[half, :, :, block]
                copy = remote(part, part, zs.at[i, step], zr.at[i, step], at(x, y, up if way == 0 else down, t))
                copy.start()
                sent.append(copy)

    def arrive(step):
        for i, (half, way, hops) in enumerate(streams):
            if step < hops:
                block = (z + NZ - step - 1) % NZ if way == 0 else (z + step + 1) % NZ
                part = kva.at[half, :, :, block]
                remote(
                    part, part, zs.at[i, step], zr.at[i, step], at(x, y, up if way == 0 else down, t)
                ).wait_recv()

    hop(0)
    half = ROWS // 2
    to_right.wait_recv()
    on_right = remote(
        qa.at[1, 0:half], qa.at[2, 0:half], qs.at[2], qr.at[2], at(right, y, z, t)
    )
    on_right.start()
    to_left.wait_recv()
    on_left = remote(
        qa.at[3, half:ROWS], qa.at[2, half:ROWS], qs.at[3], qr.at[3], at(left, y, z, t)
    )
    on_left.start()
    for step in range(3):
        arrive(step)
        hop(step + 1)
    remote(do, doa.at[far], ds.at[0], dr.at[0], at(x, y, z, far)).wait_recv()
    on_do = remote(doa.at[far], doa.at[far], ds.at[2], dr.at[2], at(x, y, z, partner))
    on_do.start()
    arrive(3)
    on_right.wait_recv()
    on_left.wait_recv()
    remote(do, doa.at[partner], ds.at[1], dr.at[1], at(x, y, z, partner)).wait_recv()
    other = (partner + 2) % 4
    remote(doa.at[other], doa.at[other], ds.at[2], dr.at[2], at(x, y, z, partner)).wait_recv()
    for copy in plane + sent + [far_do, near_do, to_right, to_left, on_right, on_left, on_do]:
        copy.wait_send()
    own_do.wait()
    own_q.wait()


def gather(q, kv, do):
    dma = pltpu.SemaphoreType.DMA
    return pl.pallas_call(
        gather_kernel,
        out_shape=(
            jax.ShapeDtypeStruct((NX, ROWS, HD), BF16),
            jax.ShapeDtypeStruct((2, NX, NY, NZ, SUB, HD), BF16),
            jax.ShapeDtypeStruct((4, *do.shape), BF16),
        ),
        in_specs=[pl.BlockSpec(memory_space=VMEM)] * 3,
        out_specs=(pl.BlockSpec(memory_space=ANY),) * 3,
        scratch_shapes=[
            dma((4,)), dma((4,)), dma((7,)), dma((7,)), dma((4, 4)), dma((4, 4)), dma((3,)), dma((3,)), dma((3,)),
        ],
        compiler_params=pltpu.CompilerParams(collective_id=0, has_side_effects=True),
        name="gather",
    )(q, kv, do)


def swap_kernel(st, ox, sta, oxa, ss, sr, os_, or_):
    x, y, z, t = place()
    meet([at((x + dx) % NX, y, z, t) for dx in range(1, NX)])
    copies = []
    for e in range(1, NX):
        to = at((x + NX - e) % NX, y, z, t)
        copies.append(remote(st, sta.at[e], ss.at[e], sr.at[e], to))
        copies.append(remote(ox.at[e], oxa.at[e], os_.at[e], or_.at[e], to))
    for copy in copies:
        copy.start()
    for copy in copies:
        copy.wait_recv()
    for copy in copies:
        copy.wait_send()


def swap(st, ox):
    dma = pltpu.SemaphoreType.DMA
    return pl.pallas_call(
        swap_kernel,
        out_shape=(jax.ShapeDtypeStruct((NX, *st.shape), st.dtype), jax.ShapeDtypeStruct(ox.shape, BF16)),
        in_specs=[pl.BlockSpec(memory_space=VMEM), pl.BlockSpec(memory_space=ANY)],
        out_specs=(pl.BlockSpec(memory_space=ANY),) * 2,
        scratch_shapes=[dma((4,))] * 4,
        compiler_params=pltpu.CompilerParams(collective_id=1, has_side_effects=True),
        name="swap",
    )(st, ox)


def reduce_kernel(dq, g, mix, dqa, kvp, m_near, m_far, b0, b1, b2, b3, total, m_sum,
                  qs, qr, zs, zr, ks, kr, ms, mr, ls):
    x, y, z, t = place()
    up, down = (z + 1) % NZ, (z + NZ - 1) % NZ
    partner, far = t + 1 - 2 * (t % 2), (t + 2) % 4
    meet(
        [at((x + dx) % NX, (y + dy) % NY, z, t) for dx, dy in PLANE]
        + [at(x, y, up, t), at(x, y, down, t), at(x, y, z, partner), at(x, y, z, far)]
    )
    sent = []

    def send(copy):
        copy.start()
        sent.append(copy)
        return copy

    streams = [(0, 0, 4, b0), (1, 1, 4, b1), (0, 1, 3, b2), (1, 0, 3, b3)]

    def hop(step):
        for i, (half, way, hops, buf) in enumerate(streams):
            if step < hops:
                away = hops - step
                block = (z + away) % NZ if way == 0 else (z + NZ - away) % NZ
                src = g.at[half, :, :, block]
                if step > 0:
                    remote(buf.at[step - 1], buf.at[step - 1], zs.at[i, step - 1], zr.at[i, step - 1],
                           at(x, y, up if way == 0 else down, t)).wait_recv()
                    buf[step - 1] = (buf[step - 1].astype(F32) + g[half, :, :, block].astype(F32)).astype(BF16)
                    src = buf.at[step - 1]
                send(remote(src, buf.at[step], zs.at[i, step], zr.at[i, step],
                            at(x, y, up if way == 0 else down, t)))

    hop(0)
    other = (partner + 2) % 4
    near = [
        send(remote(mix.at[partner], m_near.at[0], ms.at[0], mr.at[0], at(x, y, z, partner))),
        send(remote(mix.at[other], m_near.at[1], ms.at[1], mr.at[1], at(x, y, z, partner))),
    ]
    queries = [
        send(remote(dq.at[e], dqa.at[e], qs.at[e], qr.at[e], at((x + NX - e) % NX, y, z, t)))
        for e in range(1, NX)
    ]
    near[1].wait_recv()
    m_sum[...] = (mix[far].astype(F32) + m_near[1].astype(F32)).astype(BF16)
    away = send(remote(m_sum, m_far, ms.at[2], mr.at[2], at(x, y, z, far)))
    for step in range(1, 4):
        hop(step)
    for i, (half, way, hops, buf) in enumerate(streams):
        remote(buf.at[hops - 1], buf.at[hops - 1], zs.at[i, hops - 1], zr.at[i, hops - 1],
               at(x, y, up if way == 0 else down, t)).wait_recv()
    total[0] = (b0[3].astype(F32) + b2[2].astype(F32) + g[0, :, :, z].astype(F32)).astype(BF16)
    total[1] = (b1[3].astype(F32) + b3[2].astype(F32) + g[1, :, :, z].astype(F32)).astype(BF16)
    landed = []
    for i, (dx, dy) in enumerate(PLANE):
        tx, ty = (x + dx) % NX, (y + dy) % NY
        fx, fy = (x + NX - dx) % NX, (y + NY - dy) % NY
        send(remote(total.at[:, tx, ty], kvp.at[:, x, y], ks.at[i], kr.at[i], at(tx, ty, z, t)))
        landed.append(remote(total.at[:, tx, ty], kvp.at[:, fx, fy], ks.at[i], kr.at[i], at(tx, ty, z, t)))
    own = pltpu.make_async_copy(total.at[:, x, y], kvp.at[:, x, y], ls.at[0])
    own.start()
    for copy in queries + [near[0], away] + landed:
        copy.wait_recv()
    for copy in sent:
        copy.wait_send()
    own.wait()


def reduce(dq, g, mix):
    dma = pltpu.SemaphoreType.DMA
    width = mix.shape[2]
    block = (NX, NY, SUB, HD)
    return pl.pallas_call(
        reduce_kernel,
        out_shape=(
            jax.ShapeDtypeStruct(dq.shape, BF16),
            jax.ShapeDtypeStruct((2, *block), BF16),
            jax.ShapeDtypeStruct((2, 64, width), BF16),
            jax.ShapeDtypeStruct((64, width), BF16),
        ),
        in_specs=[pl.BlockSpec(memory_space=ANY)] + [pl.BlockSpec(memory_space=VMEM)] * 2,
        out_specs=(
            pl.BlockSpec(memory_space=ANY), pl.BlockSpec(memory_space=ANY),
            pl.BlockSpec(memory_space=VMEM), pl.BlockSpec(memory_space=ANY),
        ),
        scratch_shapes=[
            pltpu.VMEM((4, *block), BF16), pltpu.VMEM((4, *block), BF16),
            pltpu.VMEM((3, *block), BF16), pltpu.VMEM((3, *block), BF16),
            pltpu.VMEM((2, *block), BF16), pltpu.VMEM((64, width), BF16),
            dma((4,)), dma((4,)), dma((4, 4)), dma((4, 4)), dma((7,)), dma((7,)), dma((3,)), dma((3,)), dma((1,)),
        ],
        compiler_params=pltpu.CompilerParams(
            collective_id=2, has_side_effects=True, vmem_limit_bytes=60 << 20
        ),
        name="reduce",
    )(dq, g, mix)


def begin_of(position, lengths):
    end, first = jnp.int32(0), jnp.zeros_like(position)
    for j in range(lengths.shape[0]):
        end = end + lengths[j]
        first = jnp.where(position >= end, end, first)
    return first


def tiles_of(r, x, y, z, lengths):
    s = ((x + NX - r) % NX) * (NY * NZ) + y * NZ + z
    start = s * TOK
    f = begin_of(start, lengths) // TOK
    q_pos = start + lax.broadcasted_iota(jnp.int32, (1, ROWS), 1) // GROUP
    low = begin_of(q_pos, lengths)
    low_most = begin_of(start + TOK - 1, lengths)
    count = (s - f) // RUNS + 1

    def tile(i):
        want = f + RUNS * i
        a = jnp.minimum(want, SHARDS - RUNS)
        base = a * TOK + x * SUB
        whole = (a == want) & (base >= low_most) & (base + (RUNS - 1) * TOK + SUB - 1 <= start)
        return a, base, want * TOK, whole

    return count, tile, q_pos, low


def seen(base, floor, q_pos, low, cols):
    i = lax.broadcasted_iota(jnp.int32, (TILE, CHUNK), 0)
    k_pos = base + i + (i // SUB) * (TOK - SUB)
    return (k_pos >= jnp.maximum(low[:, cols], floor)) & (k_pos <= q_pos[:, cols])


def forward_kernel(lengths, q, kv, out, ml, m, l, acc):
    x, y, z, _ = place()

    def shard(r, _):
        count, tile, q_pos, low = tiles_of(r, x, y, z, lengths)
        m[...] = jnp.full(m.shape, FLOOR, F32)
        l[...] = jnp.zeros(l.shape, F32)
        acc[...] = jnp.zeros(acc.shape, F32)

        def step(i, _):
            a, base, floor, whole = tile(i)
            rows = pl.ds(pl.multiple_of(a * SUB, SUB), TILE)

            def work(masked):
                k, v = kv[0, rows, :], kv[1, rows, :]
                for c in range(ROWS // CHUNK):
                    cols = slice(c * CHUNK, (c + 1) * CHUNK)
                    s = lax.dot_general(k, q[r, cols, :], NT, preferred_element_type=F32) * (SCALE * LOG2E)
                    if masked:
                        s = jnp.where(seen(base, floor, q_pos, low, cols), s, LOW)
                    old = m[:, cols]
                    new = jnp.maximum(old, jnp.max(s, axis=0, keepdims=True))
                    p = jnp.exp2(s - new)
                    shrink = jnp.exp2(old - new)
                    m[:, cols] = new
                    l[:, cols] = l[:, cols] * shrink + jnp.sum(p, axis=0, keepdims=True)
                    acc[:, cols] = acc[:, cols] * shrink + lax.dot_general(
                        v, p.astype(BF16), TN, preferred_element_type=F32
                    )

            pl.when(whole)(lambda: work(False))
            pl.when(jnp.logical_not(whole))(lambda: work(True))
            return 0

        lax.fori_loop(0, count, step, 0)
        total = l[...]
        out[r] = (acc[...] / jnp.where(total > 0, total, 1.0)).T.astype(BF16)
        ml[pl.ds(r, 1), :] = m[...]
        ml[pl.ds(r + NX, 1), :] = total
        return 0

    lax.fori_loop(0, NX, shard, 0)


def forward(lengths, q, kv):
    return pl.pallas_call(
        forward_kernel,
        out_shape=(jax.ShapeDtypeStruct((NX, ROWS, HD), BF16), jax.ShapeDtypeStruct((2 * NX, ROWS), F32)),
        in_specs=[pl.BlockSpec(memory_space=SMEM)] + [pl.BlockSpec(memory_space=VMEM)] * 2,
        out_specs=(pl.BlockSpec(memory_space=VMEM),) * 2,
        scratch_shapes=[pltpu.VMEM((1, ROWS), F32), pltpu.VMEM((1, ROWS), F32), pltpu.VMEM((HD, ROWS), F32)],
        compiler_params=pltpu.CompilerParams(vmem_limit_bytes=60 << 20),
        cost_estimate=pl.CostEstimate(flops=4 * 12 * TILE * ROWS * HD, transcendentals=12 * TILE * ROWS, bytes_accessed=8 << 20),
        name="forward",
    )(lengths, q, kv)


def backward_kernel(lengths, q, g, kv, st, sta, dq, dkv, acc, dqt, lse, delta):
    x, y, z, _ = place()
    for r in range(NX):
        tops, sums, parts = [], [], []
        for e in range(NX):
            k = (r + e) % NX
            rows = st if e == 0 else sta.at[e]
            tops.append(rows[k : k + 1, :])
            sums.append(rows[NX + k : NX + k + 1, :])
            parts.append(rows[2 * NX + k : 2 * NX + k + 1, :])
        top = jnp.maximum(jnp.maximum(tops[0], tops[1]), jnp.maximum(tops[2], tops[3]))
        weights = [jnp.exp2(a - top) * b for a, b in zip(tops, sums)]
        total = (weights[0] + weights[1]) + (weights[2] + weights[3])
        lse[r : r + 1, :] = top + jnp.log2(total)
        delta[r : r + 1, :] = sum(w * b for w, b in zip(weights, parts)) / total
    acc[...] = jnp.zeros(acc.shape, F32)

    def shard(r, _):
        count, tile, q_pos, low = tiles_of(r, x, y, z, lengths)
        dqt[...] = jnp.zeros(dqt.shape, F32)

        def step(i, _):
            a, base, floor, whole = tile(i)
            rows = pl.ds(pl.multiple_of(a * SUB, SUB), TILE)

            def work(masked):
                k, v = kv[0, rows, :], kv[1, rows, :]
                dk, dv = acc[0, rows, :], acc[1, rows, :]
                for c in range(ROWS // CHUNK):
                    cols = slice(c * CHUNK, (c + 1) * CHUNK)
                    qc, gc = q[r, cols, :], g[r, cols, :]
                    s = lax.dot_general(k, qc, NT, preferred_element_type=F32) * (SCALE * LOG2E)
                    p = jnp.exp2(s - lse[pl.ds(r, 1), cols])
                    if masked:
                        p = jnp.where(seen(base, floor, q_pos, low, cols), p, 0.0)
                    dp = lax.dot_general(v, gc, NT, preferred_element_type=F32)
                    ds = (p * (dp - delta[pl.ds(r, 1), cols])).astype(BF16)
                    dv = dv + lax.dot_general(p.astype(BF16), gc, NN, preferred_element_type=F32)
                    dk = dk + lax.dot_general(ds, qc, NN, preferred_element_type=F32)
                    dqt[:, cols] = dqt[:, cols] + lax.dot_general(k, ds, TN, preferred_element_type=F32)
                acc[0, rows, :] = dk
                acc[1, rows, :] = dv

            pl.when(whole)(lambda: work(False))
            pl.when(jnp.logical_not(whole))(lambda: work(True))
            return 0

        lax.fori_loop(0, count, step, 0)
        dq[r] = (dqt[...] * SCALE).T.astype(BF16)
        return 0

    lax.fori_loop(0, NX, shard, 0)
    dkv[0] = (acc[0] * SCALE).astype(BF16)
    dkv[1] = acc[1].astype(BF16)


def backward(lengths, q, g, kv, st, sta):
    return pl.pallas_call(
        backward_kernel,
        out_shape=(jax.ShapeDtypeStruct(q.shape, BF16), jax.ShapeDtypeStruct(kv.shape, BF16)),
        in_specs=[pl.BlockSpec(memory_space=SMEM)] + [pl.BlockSpec(memory_space=VMEM)] * 5,
        out_specs=(pl.BlockSpec(memory_space=VMEM),) * 2,
        scratch_shapes=[
            pltpu.VMEM(kv.shape, F32), pltpu.VMEM((HD, ROWS), F32),
            pltpu.VMEM((NX, ROWS), F32), pltpu.VMEM((NX, ROWS), F32),
        ],
        compiler_params=pltpu.CompilerParams(vmem_limit_bytes=60 << 20),
        cost_estimate=pl.CostEstimate(flops=10 * 12 * TILE * ROWS * HD, transcendentals=12 * TILE * ROWS, bytes_accessed=10 << 20),
        name="backward",
    )(lengths, q, g, kv, st, sta)


def local(queries, keys, values, w_out, d_out, lengths):
    width = w_out.shape[2]
    kv = jnp.stack([keys.reshape(NX, SUB, HD), values.reshape(NX, SUB, HD)])
    qa, kva, doa = gather(queries.reshape(ROWS, HD), kv, d_out)
    w_flat = w_out.reshape(GROUP * HD, width)
    g = lax.dot_general(doa.reshape(TOK, width), w_flat, NT, preferred_element_type=F32)
    g = g.astype(BF16).reshape(ROWS, HD)
    outer = NX * NY
    ga = [g] + [
        lax.ppermute(g, "outer", [(i, (i + NY * e) % outer) for i in range(outer)]) for e in range(1, NX)
    ]
    ga = jnp.stack(ga)
    kva = kva.reshape(2, SHARDS * SUB, HD)
    ox, ml = forward(lengths, qa, kva)
    parts = jnp.sum(ga.astype(F32) * ox.astype(F32), axis=2)
    st = jnp.concatenate([ml, parts, jnp.zeros_like(parts)], axis=0)
    sta, oxa = swap(st, ox)
    tops = jnp.stack([st[0]] + [sta[e, e] for e in range(1, NX)])
    sums = jnp.stack([st[NX]] + [sta[e, NX + e] for e in range(1, NX)])
    weights = jnp.exp2(tops - jnp.max(tops, axis=0, keepdims=True)) * sums
    weights = weights / jnp.sum(weights, axis=0, keepdims=True)
    attn = weights[0][:, None] * ox[0].astype(F32)
    for e in range(1, NX):
        attn = attn + weights[e][:, None] * oxa[e].astype(F32)
    attn = attn.astype(BF16).reshape(TOK, GROUP * HD)
    mix = jnp.dot(attn, w_flat, preferred_element_type=F32).astype(BF16).reshape(4, TOK // 4, width)
    dq, dkv = backward(lengths, qa, ga, kva, st, sta)
    dqa, kvp, m_near, m_far = reduce(dq, dkv.reshape(2, NX, NY, NZ, SUB, HD), mix)
    mine = lax.dynamic_index_in_dim(mix, lax.axis_index("tensor"), 0, keepdims=False)
    mixed = (mine.astype(F32) + m_near[0].astype(F32) + m_far.astype(F32)).astype(BF16)
    d_queries = dq[0].astype(F32)
    for e in range(1, NX):
        d_queries = d_queries + dqa[e].astype(F32)
    d_queries = d_queries.astype(BF16).reshape(TOK, GROUP, HD)
    d_kv = (kvp[:, :, 0].astype(F32) + kvp[:, :, 1].astype(F32)).astype(BF16)
    return (mixed, d_queries, d_kv[0].reshape(TOK, 1, HD), d_kv[1].reshape(TOK, 1, HD))


def solution(mesh):
    tokens = P(("outer", "inner"), "tensor", None)
    rows = P(("outer", "inner", "tensor"), None)
    return jax.shard_map(
        local,
        mesh=mesh,
        in_specs=(tokens, tokens, tokens, P("tensor", None, None), rows, P()),
        out_specs=(rows, tokens, tokens, tokens),
        check_vma=False,
    )
```

time: 1240 us -> 180 us (0.15)
  waiting for transfers between devices: 1170 us -> 0.01 us
  Pallas kernels: 0 us -> 151 us
  loops' own time: 22.2 us -> 0 us
  between operations: 13.9 us -> 0.83 us
  matrix products: 21.9 us -> 9.27 us
    all_gather x3 -> x0, waiting for transfers between devices: 587 us -> none  [the longest x1 302 us: local(): lax.all_gather(values, ('outer', 'inner'), axis=0, tiled=True)]
    reduce_scatter x2 -> x0, waiting for transfers between devices: 578 us -> none  [the longest x1 492 us: local(): lax.psum_scatter(key_terms, ('outer', 'inner'), scatter_dimension=0, tile...]
    pallas_call x0 -> x5, Pallas kernels: none -> 151 us  [the longest x1 52.6 us: reduce(): pl.pallas_call(reduce_kernel, out_shape=(jax.ShapeDtypeStruct(dq.shape, B...]
    another operation x34 -> x0, loops' own time: 22.2 us -> none  [the longest x1 10.8 us: local(): top, denom, acc = lax.fori_loop(0, n_blocks, forward_block, start_state)]
    dot_general x9 -> x2, matrix products: 21.9 us -> 9.27 us  [the longest x1 5.16 us: local(): jnp.dot(attn, w_flat, preferred_element_type=F32).astype(BF16)]
  transfers between devices with their start and end apart: 5 -> 3, of which waited for: 5 -> 0; matrix products, arithmetic and copies ran while one was open for 1% -> 1% of each run, Pallas kernels for 0% -> 11%
where the time goes in v1:
time: 180 us; the launch traced here: 177 us
  Pallas kernels  151 us (84%)
  other arithmetic  11.2 us (6%)
  matrix products  9.27 us (5%)
  local copies, waits for them, and re-layouts  2.86 us (2%)
  starting transfers between devices  1.83 us (1%)
    pallas_call x1, Pallas kernels, reduce(): pl.pallas_call(reduce_kernel, out_shape=(jax.ShapeDtypeStruct(dq.shape, B...  52.6 us
    pallas_call x1, Pallas kernels, gather(): pl.pallas_call(gather_kernel, out_shape=(jax.ShapeDtypeStruct((NX, ROWS,...  41.3 us
    pallas_call x1, Pallas kernels, swap(): pl.pallas_call(swap_kernel, out_shape=(jax.ShapeDtypeStruct((NX, *st.shap...  19.6 us
    pallas_call x1, Pallas kernels, forward(): pl.pallas_call(forward_kernel, out_shape=(jax.ShapeDtypeStruct((NX, ROWS,...  19 us
    pallas_call x1, Pallas kernels, backward(): pl.pallas_call(backward_kernel, out_shape=(jax.ShapeDtypeStruct(q.shape,...  18.7 us
    dot_general x1, matrix products, local(): jnp.dot(attn, w_flat, preferred_element_type=F32).astype(BF16)  5.16 us
    dot_general x1, matrix products, local(): lax.dot_general(doa.reshape(TOK, width), w_flat, NT, preferred_element_ty...  4.11 us
  transfers between devices with their start and end apart: 3, of which 0 were waited for; matrix products, arithmetic and copies ran while one was open for 1% of the time, Pallas kernels for 11%

profile of v1, /device:TPU:1, one launch (start us, length us, event | category | flops | bytes accessed | tf_op | source)
XLA Modules:
  0.0 177.1 jit_solution(6762757166038534012)
XLA Ops:
  0.6 1.5 pad_maximum_fusion.1.kv
  2.2 41.3 %gather.1 = (bf16[4,1024,128]{2,1,0:T(8,128)(2,1)}, bf16[2,4,2,8,64,128]{5,4,3,2,1,0:T(8,128)(2,1)}, bf16[4,64,4096]{2,1,0:T(8,128)(2,1)}) custom-call(bf16[1024,128]{1,0:T(8,128)(2,1)} %bitcast.70, bf16[2,4,64,128]{3,2,1,0:T(8,128)(2,1)} %pad_maximum_fusion.1.kv, bf16[64,4096]{1,0:T(8,128)(2,1)} %do.1), custom_call_target="tpu_custom_call" | custom-call | tf_op jit(solution)/shard_map/gather/pallas_call | solution.py:142
  43.5 4.1 %convolution_convert_fusion = bf16[256,512]{1,0:T(8,128)(2,1)S(1)} fusion(bf16[256,4096]{1,0:T(8,128)(2,1)} %bitcast.79, bf16[512,4096]{1,0:T(8,128)(2,1)} %bitcast.58), kind=kOutput, calls=%fused_computation.3 | convolution fusion | flops 1073872896 | bytes 6553600 | tf_op jit(solution)/shard_map/dot_general | solution.py:452
  47.6 0.2 reshape.104
  47.8 0.1 collective-permute-start.2
  47.9 1.0 collective-permute-start.1
  48.8 0.8 collective-permute-start
  49.6 19.0 %forward.1 = (bf16[4,1024,128]{2,1,0:T(8,128)(2,1)}, f32[8,1024]{1,0:T(8,128)}) custom-call(s32[16]{0:T(128)} %lengths.3, bf16[4,1024,128]{2,1,0:T(8,128)(2,1)} %get-tuple-element.17.q, bf16[2,4096,128]{2,1,0:T(8,128)(2,1)} %bitcast.77), custom_call_target="tpu_custom_call" | custom-call | flops 1610612736 | bytes 8388608 | tf_op jit(solution)/shard_map/forward/pallas_call | solution.py:363
  68.6 0.0 copy-start
  68.6 0.2 stack_reshape.11
  68.7 0.1 pad.10.clone
  68.8 1.0 slice_convert_fusion.3
  69.9 0.0 collective-permute-done.2
  69.9 0.0 collective-permute-done.1
  69.9 0.0 collective-permute-done
  69.9 0.0 copy-start.4
  69.9 1.1 pad_maximum_fusion.g
  71.0 0.0 copy-done
  71.0 0.6 multiply_reduce_fusion
  71.7 0.0 copy-done.4
  71.7 0.7 maximum_maximum_fusion.st
  72.4 19.6 %swap.1 = (f32[4,16,1024]{2,1,0:T(8,128)}, bf16[4,1024,128]{2,1,0:T(8,128)(2,1)}) custom-call(f32[16,1024]{1,0:T(8,128)} %maximum_maximum_fusion.st, bf16[4,1024,128]{2,1,0:T(8,128)(2,1)} %get-tuple-element.21.ox), custom_call_target="tpu_custom_call" | custom-call | tf_op jit(solution)/shard_map/swap/pallas_call | solution.py:177
  92.0 0.8 fusion.17
  92.8 0.9 slice_bitcast_fusion.5
  93.6 0.0 copy-start.1
  93.7 18.7 %backward.1 = (bf16[4,1024,128]{2,1,0:T(8,128)(2,1)}, bf16[2,4096,128]{2,1,0:T(8,128)(2,1)}) custom-call(s32[16]{0:T(128)} %lengths.3, bf16[4,1024,128]{2,1,0:T(8,128)(2,1)} %get-tuple-element.17.q, bf16[4,1024,128]{2,1,0:T(8,128)(2,1)} %pad_maximum_fusion.g, bf16[2,4096,128]{2,1,0:T(8,128)(2,1)} %bitcast.78, f32[16,1024]{1,0:T(8,128)} %maximum_maximum_fusion.st, ...), custom_call_target="tpu_custom_call" | custom-call | flops 4026531840 | bytes 10485760 | tf_op jit(solution)/shard_map/backward/pallas_call | solution.py:432
  112.4 0.1 fusion.14
  112.5 0.1 mul.56
  112.6 0.1 copy.18
  112.7 0.1 mul.65
  112.8 0.1 copy.24
  112.9 0.1 mul.62
  113.1 0.1 copy.22
  113.1 0.1 mul.59
  113.3 0.1 copy.20
  113.4 0.0 copy-done.1
  113.4 0.1 slice_convert_fusion.2
  113.5 5.2 %fusion = bf16[256,4096]{1,0:T(8,128)(2,1)} fusion(bf16[4,128,4096]{2,1,0:T(8,128)(2,1)} %param.9, f32[256,4,128]{2,1,0:T(4,128)S(1)} %bitcast.62, f32[256,4,128]{2,1,0:T(4,128)S(1)} %bitcast.63, f32[256,4,128]{2,1,0:T(4,128)S(1)} %bitcast.61, f32[256,4,128]{2,1,0:T(4,128)S(1)} %bitcast.59, f32[256,4]{0,1:T(4,128)S(1)} %copy.24, f32[256,4]{0,1:T(4,128)S(1)} %copy.22, ...), kind=kOutput, calls=%fused_computation.1 | convolution fusion | flops 1075838976 | bytes 8404992 | tf_op jit(solution)/shard_map/dot_general | solution.py:472
  118.7 52.6 %reduce.21 = (bf16[4,1024,128]{2,1,0:T(8,128)(2,1)}, bf16[2,4,2,64,128]{4,3,2,1,0:T(8,128)(2,1)}, bf16[2,64,4096]{2,1,0:T(8,128)(2,1)}, bf16[64,4096]{1,0:T(8,128)(2,1)}) custom-call(bf16[4,1024,128]{2,1,0:T(8,128)(2,1)} %get-tuple-element.24.dq, bf16[2,4,2,8,64,128]{5,4,3,2,1,0:T(8,128)(2,1)} %bitcast.60, bf16[4,64,4096]{2,1,0:T(8,128)(2,1)} %bitcast.56), custom_call_target="tpu_custom_call" | custom-call | tf_op jit(solution)/shard_map/reduce/pallas_call | solution.py:259
  171.2 0.0 copy-start.2
  171.2 0.0 copy-start.3
  171.2 2.1 %add_convert_fusion = bf16[1,1024,128]{2,1,0:T(8,128)(2,1)} fusion(bf16[4,1024,128]{2,1,0:T(8,128)(2,1)} %get-tuple-element.28, bf16[4,1024,128]{2,1,0:T(8,128)(2,1)} %get-tuple-element.24.dq), kind=kLoop, calls=%fused_computation.15 | loop fusion | flops 1048576 | bytes 1310720 | tf_op jit(solution)/shard_map/convert.4
  173.4 1.0 add_convert_fusion.1
  174.4 0.7 fusion.16
  175.1 0.0 copy-done.2
  175.1 0.0 copy-done.3
  175.1 2.0 %fusion.1 = bf16[64,4096]{1,0:T(8,128)(2,1)} fusion(bf16[64,4096]{1,0:T(8,128)(2,1)S(1)} %copy-done.2, bf16[2,64,4096]{2,1,0:T(8,128)(2,1)S(1)} %copy-done.3, bf16[4,64,4096]{2,1,0:T(8,128)(2,1)} %bitcast.57, s32[]{:T(128)S(6)} %select_n.4), kind=kLoop, calls=%fused_computation.6 | loop fusion | flops 1572864 | bytes 2097156 | tf_op jit(solution)/shard_map/convert_element_type | solution.py:476
  (3 shorter events, 0.1 us)
Async XLA Ops:
  47.8 22.1 %collective-permute-start.2 = (bf16[1024,128]{1,0:T(8,128)(2,1)S(1)}, bf16[1024,128]{1,0:T(8,128)(2,1)S(1)}, u32[]{:S(2)}, u32[]{:S(2)}) collective-permute-start(bf16[1024,128]{1,0:T(8,128)(2,1)S(1)} %reshape.104), channel_id=1, source_target_pairs={{0,192},{32,224},{64,0},{96,32},{128,64},{160,96},{192,128},{224,1... | collective-permute-start | bytes 786440 | tf_op jit(solution)/shard_map/ppermute | solution.py:456
  47.9 22.0 %collective-permute-start.1 = (bf16[1024,128]{1,0:T(8,128)(2,1)S(1)}, bf16[1024,128]{1,0:T(8,128)(2,1)S(1)}, u32[]{:S(2)}, u32[]{:S(2)}) collective-permute-start(bf16[1024,128]{1,0:T(8,128)(2,1)S(1)} %reshape.104), channel_id=1, source_target_pairs={{0,128},{32,160},{64,192},{96,224},{128,0},{160,32},{192,64},{224,... | collective-permute-start | bytes 786440 | tf_op jit(solution)/shard_map/ppermute | solution.py:456
  48.8 21.1 %collective-permute-start = (bf16[1024,128]{1,0:T(8,128)(2,1)S(1)}, bf16[1024,128]{1,0:T(8,128)(2,1)S(1)}, u32[]{:S(2)}, u32[]{:S(2)}) collective-permute-start(bf16[1024,128]{1,0:T(8,128)(2,1)S(1)} %reshape.104), channel_id=1, source_target_pairs={{0,64},{32,96},{64,128},{96,160},{128,192},{160,224},{192,0},{224,... | collective-permute-start | bytes 786440 | tf_op jit(solution)/shard_map/ppermute | solution.py:456
  68.6 2.5 %copy-start = (bf16[4,1024,128]{2,1,0:T(8,128)(2,1)S(1)}, bf16[4,1024,128]{2,1,0:T(8,128)(2,1)}, u32[]{:S(2)}) copy-start(bf16[4,1024,128]{2,1,0:T(8,128)(2,1)} %get-tuple-element.21.ox) | copy-start | bytes 3145732
  69.9 1.8 %copy-start.4 = (f32[8,1024]{1,0:T(8,128)S(1)}, f32[8,1024]{1,0:T(8,128)}, u32[]{:S(2)}) copy-start(f32[8,1024]{1,0:T(8,128)} %get-tuple-element.19) | copy-start | bytes 98308
  93.6 19.7 %copy-start.1 = (bf16[4,1024,128]{2,1,0:T(8,128)(2,1)S(1)}, bf16[4,1024,128]{2,1,0:T(8,128)(2,1)}, u32[]{:S(2)}) copy-start(bf16[4,1024,128]{2,1,0:T(8,128)(2,1)} %get-tuple-element.23) | copy-start | bytes 3145732
  171.2 3.8 %copy-start.2 = (bf16[64,4096]{1,0:T(8,128)(2,1)S(1)}, bf16[64,4096]{1,0:T(8,128)(2,1)}, u32[]{:S(2)}) copy-start(bf16[64,4096]{1,0:T(8,128)(2,1)} %get-tuple-element.27) | copy-start | bytes 1572868
  171.2 3.8 %copy-start.3 = (bf16[2,64,4096]{2,1,0:T(8,128)(2,1)S(1)}, bf16[2,64,4096]{2,1,0:T(8,128)(2,1)}, u32[]{:S(2)}) copy-start(bf16[2,64,4096]{2,1,0:T(8,128)(2,1)} %get-tuple-element.26) | copy-start | bytes 3145732
